TPU v7x, 32 devices: a whole 2x2x4 slice. The times are simulated.
32 devices in a mesh: seq: 4 (over y, x), head: 4 (over z), rep: 2 (over core).
Axes of the slice: x: 2, y: 2, z: 4, core: 2. Of those that a mesh axis runs over, the one named last changes fastest.
Arguments:
- query_heads: bfloat16 [2, 8192, 4096], P('rep', 'seq', 'head'), may hold values from -0.59765625 to 0.59765625
- key_heads: bfloat16 [2, 8192, 4096], P('rep', 'seq', 'head'), may hold values from -0.59765625 to 0.59765625
- value_heads: bfloat16 [2, 8192, 4096], P('rep', 'seq', 'head'), may hold values from -6 to 6
- out_cotangent: bfloat16 [2, 8192, 4096], P('rep', 'seq', 'head'), may hold values from -0.19921875 to 0.19921875
- out_weight: bfloat16 [4096, 4096], P('head'), may hold values from -0.09375 to 0.09375
- doc_ends: int32 [2, 7], P('rep'), may hold values from 1 to 8192, as said below
Outputs:
- grad_query: bfloat16 [2, 8192, 4096], P('rep', 'seq', 'head')
- grad_key: bfloat16 [2, 8192, 4096], P('rep', 'seq', 'head')
- grad_value: bfloat16 [2, 8192, 4096], P('rep', 'seq', 'head')
- grad_weight: float32 [4096, 4096], P('head', ('seq', 'rep'))
Inputs may be any that keep to these rules, and one draw needn't show every extreme that they name: `doc_ends`: each row holds 7 strictly increasing document end offsets; its last entry is 8192.
All inputs are finite; a program needn't handle non-finite values.
Results may differ from a plain program's by a relative error of at most 0.0052.
Values may be sent and summed in bfloat16 or wider, within the bound.
No kernel may reach another device: no remote copies, remote signals or barrier semaphores. Data moves between devices by JAX's collectives and lax.ppermute only.
A program may use at most 320 MiB of HBM per device.

v0:
```python
import jax
import jax.numpy as jnp
from jax import lax
from jax.sharding import PartitionSpec as P

HD = 128
BLOCK = 512


highest = lax.Precision.HIGHEST


def prefix(shard, axis, combine, identity, reverse):
    count, here = (lax.axis_size(axis), lax.axis_index(axis))
    everything = jax.tree.map(lambda part: lax.all_gather(part, axis), shard)
    start = jax.tree.map(
        lambda part, zero: jnp.broadcast_to(jnp.asarray(zero, part.dtype), part.shape),
        shard,
        identity,
    )

    def step(k, before):
        at = count - 1 - k if reverse else k
        reached = at > here if reverse else at < here
        new = combine(before, jax.tree.map(lambda part: part[at], everything))
        return jax.tree.map(lambda a, b: jnp.where(reached, a, b), new, before)

    return lax.fori_loop(0, count, step, start)


def doc_counts(positions, ends_row):
    return jnp.sum((ends_row[None, :] <= positions[:, None]).astype(jnp.int32), axis=1)


def local_pass(queries, keys, values, grads, counts, count_before):
    length, heads, width = queries.shape
    blocks = length // BLOCK
    query_blocks = queries.reshape(blocks, BLOCK, heads, width)
    key_blocks = keys.reshape(blocks, BLOCK, heads, width)
    value_blocks = values.reshape(blocks, BLOCK, heads, width)
    grad_blocks = grads.reshape(blocks, BLOCK, heads, width)
    count_blocks = counts.reshape(blocks, BLOCK)
    before_each = jnp.concatenate([jnp.reshape(count_before, (1,)), count_blocks[:-1, -1]])
    last_each = count_blocks[:, -1]
    rows = lax.broadcasted_iota(jnp.int32, (BLOCK, BLOCK), 0)
    cols = lax.broadcasted_iota(jnp.int32, (BLOCK, BLOCK), 1)
    allowed = (
        (count_blocks[:, :, None] == count_blocks[:, None, :]) & (rows >= cols)[None]
    ).astype(jnp.float32)
    scores = jnp.einsum(
        "nthe,nshe->nhts", query_blocks, key_blocks, preferred_element_type=jnp.float32
    )
    attn = (scores * allowed[:, None]).astype(jnp.bfloat16)
    back = jnp.einsum(
        "nthe,nshe->nhts", grad_blocks, value_blocks, preferred_element_type=jnp.float32
    )
    pgrad = (back * allowed[:, None]).astype(jnp.bfloat16)
    out_intra = jnp.einsum(
        "nhts,nshe->nthe", attn, value_blocks, preferred_element_type=jnp.float32
    )
    dq_intra = jnp.einsum("nhts,nshe->nthe", pgrad, key_blocks, preferred_element_type=jnp.float32)
    dk_intra = jnp.einsum(
        "nhts,nthe->nshe", pgrad, query_blocks, preferred_element_type=jnp.float32
    )
    dv_intra = jnp.einsum("nhts,nthe->nshe", attn, grad_blocks, preferred_element_type=jnp.float32)
    first_match = (count_blocks == before_each[:, None])[:, :, None, None]
    last_match = (count_blocks == last_each[:, None])[:, :, None, None]
    keep = (last_each == before_each).astype(jnp.float32)
    tails = jnp.einsum(
        "nshe,nshf->nhef",
        key_blocks * last_match.astype(jnp.bfloat16),
        value_blocks,
        preferred_element_type=jnp.float32,
    )
    head_sums = jnp.einsum(
        "nthe,nthf->nhef",
        query_blocks * first_match.astype(jnp.bfloat16),
        grad_blocks,
        preferred_element_type=jnp.float32,
    )

    def link_step(state, item):
        return (item[0] + item[1] * state, state)

    empty = jnp.zeros((heads, width, width), jnp.float32)
    final_tail, states_before = lax.scan(link_step, empty, (tails, keep))
    final_head, states_after = lax.scan(link_step, empty, (head_sums, keep), reverse=True)
    first_weight = first_match.astype(jnp.float32)
    last_weight = last_match.astype(jnp.float32)
    outputs = out_intra + first_weight * jnp.einsum(
        "nthe,nhef->nthf", query_blocks.astype(jnp.float32), states_before, precision=highest
    )
    dq = dq_intra + first_weight * jnp.einsum(
        "nthf,nhef->nthe", grad_blocks.astype(jnp.float32), states_before, precision=highest
    )
    dk = dk_intra + last_weight * jnp.einsum(
        "nshf,nhef->nshe", value_blocks.astype(jnp.float32), states_after, precision=highest
    )
    dv = dv_intra + last_weight * jnp.einsum(
        "nshe,nhef->nshf", key_blocks.astype(jnp.float32), states_after, precision=highest
    )
    shape = (length, heads, width)
    return (
        outputs.reshape(shape),
        dq.reshape(shape),
        dk.reshape(shape),
        dv.reshape(shape),
        final_tail,
        final_head,
    )


def link_states(earlier, later):
    return (jnp.maximum(earlier[0], later[0]), later[1] + (1.0 - later[0]) * earlier[1])


def on_device(query_heads, key_heads, value_heads, out_cotangent, out_weight, doc_ends):
    length = query_heads.shape[1]
    heads = query_heads.shape[2] // HD
    queries = query_heads[0].reshape(length, heads, HD)
    keys = key_heads[0].reshape(length, heads, HD)
    values = value_heads[0].reshape(length, heads, HD)
    full_cotangent = lax.all_gather(out_cotangent, "head", axis=2, tiled=True)[0]
    grads_flat = lax.dot_general(
        full_cotangent, out_weight, (((1,), (1,)), ((), ())), preferred_element_type=jnp.float32
    ).astype(jnp.bfloat16)
    grads = grads_flat.reshape(length, heads, HD)
    offset = lax.axis_index("seq") * length
    positions = offset + jnp.arange(length, dtype=jnp.int32)
    ends_row = doc_ends[0]
    counts = doc_counts(positions, ends_row)
    count_before = doc_counts(jnp.reshape(offset - 1, (1,)), ends_row)[0]
    outputs, dq, dk, dv, tail, head = local_pass(queries, keys, values, grads, counts, count_before)
    flag = (counts[-1] != count_before).astype(jnp.float32)
    identity = (jnp.zeros((), jnp.float32), jnp.zeros_like(tail))
    flag_before, carry_before = prefix((flag, tail), "seq", link_states, identity, False)
    flag_after, carry_after = prefix((flag, head), "seq", link_states, identity, True)
    entry_weight = (counts == count_before).astype(jnp.float32)[:, None, None]
    exit_weight = (counts == counts[-1]).astype(jnp.float32)[:, None, None]
    outputs = outputs + entry_weight * jnp.einsum(
        "the,hef->thf", queries.astype(jnp.float32), carry_before, precision=highest
    )
    dq = dq + entry_weight * jnp.einsum(
        "thf,hef->the", grads.astype(jnp.float32), carry_before, precision=highest
    )
    dk = dk + exit_weight * jnp.einsum(
        "thf,hef->the", values.astype(jnp.float32), carry_after, precision=highest
    )
    dv = dv + exit_weight * jnp.einsum(
        "the,hef->thf", keys.astype(jnp.float32), carry_after, precision=highest
    )
    flat = heads * HD
    attention_out = outputs.reshape(length, flat).astype(jnp.bfloat16)
    grad_query = dq.reshape(1, length, flat).astype(jnp.bfloat16)
    grad_key = dk.reshape(1, length, flat).astype(jnp.bfloat16)
    grad_value = dv.reshape(1, length, flat).astype(jnp.bfloat16)
    partial_grad = lax.dot_general(
        attention_out, full_cotangent, (((0,), (0,)), ((), ())), preferred_element_type=jnp.float32
    )
    summed = lax.psum(partial_grad, ("seq", "rep"))
    columns = summed.shape[1] // lax.axis_size(("seq", "rep"))
    grad_weight = lax.dynamic_slice_in_dim(
        summed, lax.axis_index(("seq", "rep")) * columns, columns, 1
    )
    return (grad_query, grad_key, grad_value, grad_weight)


def solution(mesh):
    in_specs = (
        P("rep", "seq", "head"),
        P("rep", "seq", "head"),
        P("rep", "seq", "head"),
        P("rep", "seq", "head"),
        P("head", None),
        P("rep", None),
    )
    out_specs = (
        P("rep", "seq", "head"),
        P("rep", "seq", "head"),
        P("rep", "seq", "head"),
        P("head", ("seq", "rep")),
    )
    return jax.shard_map(
        on_device, mesh=mesh, in_specs=in_specs, out_specs=out_specs, check_vma=False
    )
```

profile of v0, /device:TPU:0, one launch (start us, length us, event | category | flops | bytes accessed | tf_op | source)
XLA Modules:
  0.0 711.6 jit_solution(5314023280602779764)
XLA Ops:
  33.0 10.0 %while.60 = (s32[]{:T(128)}, f32[8,128,128]{2,1,0:T(8,128)S(1)}, f32[4,8,128,128]{3,2,1,0:T(8,128)S(1)}, f32[4,8,128,128]{3,2,1,0:T(8,128)}, f32[4]{0:T(128)S(1)}, /*index=5*/s32[]{:T(128)}, s32[]{:T(128)}) while((s32[]{:T(128)}, f32[8,128,128]{2,1,0:T(8,128)S(1)}, f32[4,8,128,128]{3,2,1,0:T(8,128)S(1)}, ...), condition=%wide.region_3.4_spmd.clone, body=%wide.region_2.3_spmd.clone.sunk | while | flops 524291 | bytes 2621560 | solution.py:86
  48.1 12.1 %all-reduce = f32[4]{0:T(128)S(1)} all-reduce(f32[4]{0:T(128)S(1)} %dynamic-update-slice), channel_id=1, replica_groups=mesh['seq'=4,'head'=4,'rep'=2] {'seq'}, use_global_device_ids=true, to_apply=%add | all-reduce | flops 4 | bytes 32
  75.7 11.6 %multiply_convert_fusion = bf16[4,8,512,512]{3,2,1,0:T(8,128)(2,1)} fusion(f32[4,512,512]{2,1,0:T(8,128)} %and_convert_fusion, bf16[4,512,8,128]{1,3,2,0:T(8,128)(2,1)} %copy.184, bf16[4,512,8,128]{1,3,2,0:T(8,128)(2,1)} %copy.175), kind=kOutput, calls=%fused_computation.8 | convolution fusion | flops 2164260864 | bytes 29360128 | tf_op jit(solution)/shard_map/nthe,nshe->nhts/dot_general | solution.py:50
  87.2 17.3 %fusion.24 = f32[4,8,512,128]{3,2,1,0:T(8,128)} fusion(bf16[4,8,512,512]{3,2,1,0:T(8,128)(2,1)} %multiply_convert_fusion, bf16[4,512,8,128]{3,2,1,0:T(8,128)(2,1)} %bitcast.138), kind=kOutput, calls=%fused_computation.39 | convolution fusion | flops 2147483648 | bytes 29360128 | tf_op jit(solution)/shard_map/nhts,nshe->nthe/dot_general | solution.py:58
  132.3 11.0 %while.61 = (s32[]{:T(128)}, f32[8,128,128]{2,1,0:T(8,128)S(1)}, s32[]{:T(128)}, f32[4,8,128,128]{3,2,1,0:T(8,128)}, f32[4]{0:T(128)S(1)}, /*index=5*/s32[]{:T(128)}, f32[1]{0:T(128)}, s32[]{:T(128)}) while((s32[]{:T(128)}, f32[8,128,128]{2,1,0:T(8,128)S(1)}, s32[]{:T(128)}, f32[4,8,128,128]{3,2,1,0:T(8,128)}, f32[4]{0:T(128)S(1)}, ...), condition=%wide.region_5.6_spmd.clone, body=%wide.region_4.5_spmd.clone.sunk | while | flops 524293 | bytes 1573009 | solution.py:28
  143.3 10.8 %fusion.6 = bf16[2048,8,128]{0,2,1:T(8,128)(2,1)} fusion(f32[2048,8,128]{0,2,1:T(8,128)} %copy.209, f32[8,128,128]{2,1,0:T(8,128)S(1)} %get-tuple-element.364, bf16[2048,8,128]{2,1,0:T(8,128)(2,1)} %bitcast.145, f32[2048]{0:T(1024)S(1)} %get-tuple-element.507), kind=kOutput, calls=%fused_computation.15 | convolution fusion | flops 3227516928 | bytes 17309696 | tf_op jit(solution)/shard_map/the,hef->thf/dot_general | solution.py:140
  154.1 216.2 %all-gather.6.cloned.1.call-done = bf16[1,2048,4096]{2,1,0:T(8,128)(2,1)} async-done(((bf16[1,2048,1024]{2,1,0:T(8,128)(2,1)}), bf16[1,2048,4096]{2,1,0:T(8,128)(2,1)}) %all-gather.6.cloned.1.call-update) | async-done | bytes 16777232 | tf_op jit(solution)/shard_map/all_gather | solution.py:123
  370.3 23.9 %fusion.17 = bf16[2048,1024]{0,1:T(8,128)(2,1)} fusion(bf16[1024,4096]{1,0:T(8,128)(2,1)} %param.18, bf16[1,2048,4096]{2,1,0:T(8,128)(2,1)} %all-gather.6.cloned.1.call-done), kind=kOutput, calls=%fused_computation.34 | convolution fusion | flops 17181966336 | bytes 29360128 | tf_op jit(solution)/shard_map/dot_general | solution.py:124
  402.1 11.7 %multiply_convert_fusion.1 = bf16[4,8,512,512]{3,2,1,0:T(8,128)(2,1)} fusion(f32[4,512,512]{2,1,0:T(8,128)} %and_convert_fusion, bf16[4,512,8,128]{1,0,3,2:T(4,128)(2,1)} %reshape_reshape.3, bf16[4,512,8,128]{3,2,1,0:T(8,128)(2,1)} %bitcast.139), kind=kOutput, calls=%fused_computation.9 | convolution fusion | flops 2164260864 | bytes 29360128 | tf_op jit(solution)/shard_map/nthe,nshe->nhts/dot_general | solution.py:54
  413.7 14.7 %fusion.34 = f32[4,8,512,128]{3,2,1,0:T(8,128)} fusion(bf16[4,8,512,512]{3,2,1,0:T(8,128)(2,1)} %multiply_convert_fusion.1, bf16[4,512,8,128]{1,3,2,0:T(8,128)(2,1)} %copy.175), kind=kOutput, calls=%fused_computation.62 | convolution fusion | flops 2147483648 | bytes 29360128 | tf_op jit(solution)/shard_map/nhts,nshe->nthe/dot_general | solution.py:61
  435.1 10.6 %while.62 = (s32[]{:T(128)}, f32[8,128,128]{2,1,0:T(8,128)S(1)}, f32[4,8,128,128]{3,2,1,0:T(8,128)S(1)}, f32[4,8,128,128]{3,2,1,0:T(8,128)}, f32[4]{0:T(128)S(1)}, /*index=5*/s32[]{:T(128)}, s32[]{:T(128)}, s32[]{:T(128)}) while((s32[]{:T(128)}, f32[8,128,128]{2,1,0:T(8,128)S(1)}, f32[4,8,128,128]{3,2,1,0:T(8,128)S(1)}, ...), condition=%wide.region_7.8_spmd.clone, body=%wide.region_6.7_spmd.clone.sunk | while | flops 524292 | bytes 2621580 | solution.py:87
  446.6 23.8 %fusion.2 = f32[1024,4096]{1,0:T(8,128)} fusion(bf16[2048,1024]{0,1:T(8,128)(2,1)} %bitcast.157, bf16[1,2048,4096]{2,1,0:T(8,128)(2,1)} %all-gather.6.cloned.1.call-done), kind=kOutput, calls=%fused_computation.10 | convolution fusion | flops 17179869184 | bytes 37748736 | tf_op jit(solution)/shard_map/dot_general | solution.py:157
  470.5 9.9 %bitcast_add_fusion.10 = f32[4,512,8,128]{3,1,2,0:T(8,128)S(1)} fusion(f32[4,8,512,128]{3,2,1,0:T(8,128)} %fusion.34, f32[4,512]{1,0:T(4,128)S(1)} %convert_element_type.133, f32[4,8,128,128]{3,2,1,0:T(8,128)} %copy-done.3, bf16[4,512,8,128]{1,0,3,2:T(4,128)(2,1)} %reshape_reshape.3), kind=kOutput, calls=%fused_computation.24 | convolution fusion | flops 3225419776 | bytes 23076864 | tf_op jit(solution)/shard_map/nthf,nhef->nthe/dot_general | solution.py:93
  488.4 10.1 %copy.181 = f32[2048,8,128]{0,2,1:T(8,128)} copy(f32[2048,8,128]{2,1,0:T(8,128)} %bitcast.147) | data formatting | bytes 16777216 | tf_op jit(solution)/shard_map/reshape | solution.py:105
  498.5 10.8 %fusion.9 = bf16[2048,8,128]{0,2,1:T(8,128)(2,1)} fusion(f32[2048,8,128]{0,2,1:T(8,128)} %copy.181, f32[8,128,128]{2,1,0:T(8,128)S(1)} %get-tuple-element.364, bf16[2048,8,128]{0,2,1:T(8,128)(2,1)} %bitcast.150, f32[2048]{0:T(1024)S(1)} %get-tuple-element.507), kind=kOutput, calls=%fused_computation.23 | convolution fusion | flops 3227516928 | bytes 17309696 | tf_op jit(solution)/shard_map/thf,hef->the/dot_general | solution.py:143
  516.0 11.7 %fusion.35 = f32[4,8,512,128]{3,2,1,0:T(8,128)} fusion(bf16[4,8,512,512]{3,2,1,0:T(8,128)(2,1)} %multiply_convert_fusion.1, bf16[4,512,8,128]{1,3,2,0:T(8,128)(2,1)} %copy.184), kind=kOutput, calls=%fused_computation.63 | convolution fusion | flops 2147483648 | bytes 29360128 | tf_op jit(solution)/shard_map/nhts,nthe->nshe/dot_general | solution.py:62
  543.8 9.4 %copy.190 = f32[2048,8,128]{0,2,1:T(8,128)} copy(f32[2048,8,128]{2,1,0:T(8,128)} %bitcast.148) | data formatting | bytes 16777216 | tf_op jit(solution)/shard_map/reshape | solution.py:106
  560.9 16.7 %add_bitcast_fusion = f32[4,512,8,128]{3,1,2,0:T(8,128)} fusion(f32[4,8,128,512]{2,3,1,0:T(8,128)} %fusion.36, f32[4,512]{1,0:T(4,128)S(1)} %copy-done.6, bf16[4,8,512,512]{3,2,1,0:T(8,128)(2,1)} %multiply_convert_fusion, bf16[4,512,8,128]{1,0,3,2:T(4,128)(2,1)} %reshape_reshape.3), kind=kOutput, calls=%fused_computation.25 | convolution fusion | flops 2151677952 | bytes 37756928 | tf_op jit(solution)/shard_map/nhts,nthe->nshe/dot_general | solution.py:65
  577.6 11.7 %copy.198 = f32[4,512,8,128]{3,2,1,0:T(8,128)} copy(f32[4,512,8,128]{3,1,2,0:T(8,128)} %add_bitcast_fusion) | data formatting | bytes 16777216 | tf_op jit(solution)/shard_map/add | solution.py:99
  589.3 9.4 %copy.201 = f32[2048,8,128]{0,2,1:T(8,128)} copy(f32[2048,8,128]{2,1,0:T(8,128)} %bitcast.149) | data formatting | bytes 16777216 | tf_op jit(solution)/shard_map/reshape | solution.py:107
  598.8 11.1 %while.63 = (s32[]{:T(128)}, f32[8,128,128]{2,1,0:T(8,128)S(1)}, s32[]{:T(128)}, f32[4,8,128,128]{3,2,1,0:T(8,128)}, f32[4]{0:T(128)S(1)}, /*index=5*/s32[]{:T(128)}, s32[]{:T(128)}, s32[]{:T(128)}, s32[]{:T(128)}, f32[1]{0:T(128)}) while((s32[]{:T(128)}, f32[8,128,128]{2,1,0:T(8,128)S(1)}, s32[]{:T(128)}, ...), condition=%wide.region_9.10_spmd.clone, body=%wide.region_8.9_spmd.clone.sunk | while | flops 524297 | bytes 1573071 | solution.py:28
  609.9 10.9 %fusion.8 = bf16[2048,8,128]{0,2,1:T(8,128)(2,1)} fusion(f32[2048,8,128]{0,2,1:T(8,128)} %copy.190, f32[8,128,128]{2,1,0:T(8,128)S(1)} %get-tuple-element.367, bf16[2048,8,128]{2,1,0:T(8,128)(2,1)} %bitcast.141, f32[2048]{0:T(1024)S(1)} %copy-done.7), kind=kOutput, calls=%fused_computation.20 | convolution fusion | flops 3227516928 | bytes 17309696 | tf_op jit(solution)/shard_map/thf,hef->the/dot_general | solution.py:146
  627.5 11.7 %fusion.7 = bf16[2048,8,128]{0,2,1:T(8,128)(2,1)} fusion(f32[2048,8,128]{0,2,1:T(8,128)} %copy.201, f32[8,128,128]{2,1,0:T(8,128)S(1)} %get-tuple-element.367, bf16[2048,8,128]{2,1,0:T(8,128)(2,1)} %bitcast.143, f32[2048]{0:T(1024)S(1)} %copy-done.7), kind=kOutput, calls=%fused_computation.18 | convolution fusion | flops 3227516928 | bytes 17309696 | tf_op jit(solution)/shard_map/the,hef->thf/dot_general | solution.py:149
  645.6 55.8 %all-reduce.3.cloned.1.call-done = f32[1024,4096]{1,0:T(8,128)} async-done(((f32[1024,4096]{1,0:T(8,128)}), f32[1024,4096]{1,0:T(8,128)}) %all-reduce.3.cloned.1.call-update) | async-done | bytes 16777232 | tf_op jit(solution)/shard_map/psum | solution.py:160
  (116 shorter events, 179.7 us)
Async XLA Ops:
  7.2 125.1 %all-gather.8.cloned.1.call-start = ((), (), s32[]{:S(2)}) async-start(), calls=%async_computation.2 | async-start | bytes 2621440 | tf_op jit(solution)/shard_map/all_gather | solution.py:15
  8.4 5.4 copy-start.5
  16.9 7.6 %copy-start.8 = (s32[1,7]{1,0:T(1,128)S(1)}, s32[1,7]{1,0:T(1,128)}, u32[]{:S(2)}) copy-start(s32[1,7]{1,0:T(1,128)} %param.19) | copy-start | bytes 88
  43.1 0.8 copy-start.1
  43.1 17.1 %copy-start.3 = (f32[4,8,128,128]{3,2,1,0:T(8,128)}, f32[4,8,128,128]{3,2,1,0:T(8,128)S(1)}, u32[]{:S(2)}) copy-start(f32[4,8,128,128]{3,2,1,0:T(8,128)S(1)} %get-tuple-element.362) | copy-start | bytes 6291460
  43.1 3.7 copy-start.11
  43.9 326.4 %all-gather.6.cloned.1.call-start = ((), (), s32[]{:S(2)}) async-start(), calls=%async_computation | async-start | bytes 20971520 | tf_op jit(solution)/shard_map/all_gather | solution.py:123
  44.6 554.1 %all-gather.10.cloned.1.call-start = ((), (), s32[]{:S(2)}) async-start(), calls=%async_computation.3 | async-start | bytes 2621440 | tf_op jit(solution)/shard_map/all_gather | solution.py:15
  87.2 17.3 %copy-start.4 = (f32[4,8,128,128]{3,2,1,0:T(8,128)S(1)}, f32[4,8,128,128]{3,2,1,0:T(8,128)}, u32[]{:S(2)}) copy-start(f32[4,8,128,128]{3,2,1,0:T(8,128)} %copy-done.3) | copy-start | bytes 6291460
  143.3 10.9 %copy-start.9 = (f32[4]{0:T(128)}, f32[4]{0:T(128)S(1)}, u32[]{:S(2)}) copy-start(f32[4]{0:T(128)S(1)} %get-tuple-element.750) | copy-start | bytes 52
  445.7 0.8 copy-start
  446.5 255.0 %all-reduce.3.cloned.1.call-start = ((), (), s32[]{:S(2)}) async-start(), calls=%async_computation.1 | async-start | bytes 33554432 | tf_op jit(solution)/shard_map/psum | solution.py:160
  516.0 11.7 %copy-start.6 = (f32[4,512]{1,0:T(4,128)S(1)}, f32[4,512]{1,0:T(4,128)}, u32[]{:S(2)}) copy-start(f32[4,512]{1,0:T(4,128)} %get-tuple-element.502) | copy-start | bytes 24580
  589.3 9.5 %copy-start.2 = (f32[8,128,128]{2,1,0:T(8,128)S(1)}, f32[8,128,128]{2,1,0:T(8,128)}, u32[]{:S(2)}) copy-start(f32[8,128,128]{2,1,0:T(8,128)} %custom-call.3) | copy-start | bytes 1572868
  589.3 9.5 %copy-start.10 = (f32[4]{0:T(128)S(1)}, f32[4]{0:T(128)}, u32[]{:S(2)}) copy-start(f32[4]{0:T(128)} %copy-done.9) | copy-start | bytes 52
  598.8 11.1 %copy-start.7 = (f32[2048]{0:T(1024)S(1)}, f32[2048]{0:T(1024)}, u32[]{:S(2)}) copy-start(f32[2048]{0:T(1024)} %get-tuple-element.506) | copy-start | bytes 24580
Sparse Core Ops, SparseCore 0:
  44.0 37.8 all-gather.7
  83.5 286.7 all-gather.5
  446.7 33.3 all-gather.9
  483.7 217.7 all-reduce.2
where the time goes:
time: 718 us; the launch traced here: 712 us
  waiting for transfers between devices  273 us (38%)
  matrix products  222 us (31%)
  local copies, waits for them, and re-layouts  148 us (21%)
  other arithmetic  34.7 us (5%)
  between operations  15.9 us (2%)
  blocking collectives  12.1 us (2%)
    all_gather x1, waiting for transfers between devices, on_device(): lax.all_gather(out_cotangent, 'head', axis=2, tiled=True)[0]  216 us
    psum x1, waiting for transfers between devices, on_device(): summed = lax.psum(partial_grad, ('seq', 'rep'))  55.8 us
    unnamed x33, local copies, waits for them, and re-layouts  36.5 us
    dot_general x1, matrix products, on_device(): lax.dot_general(full_cotangent, out_weight, (((1,), (1,)), ((), ())), pre...  23.9 us
    dot_general x1, matrix products, on_device(): lax.dot_general(attention_out, full_cotangent, (((0,), (0,)), ((), ())),...  23.8 us
    dot_general x1, matrix products, local_pass(): jnp.einsum('nhts,nshe->nthe', attn, value_blocks, preferred_element_type=...  17.3 us
    dot_general x1, matrix products, local_pass(): jnp.einsum('nhts,nthe->nshe', attn, grad_blocks, preferred_element_type=j...  16.7 us
    add x8, other arithmetic, link_step(): return (item[0] + item[1] * state, state)  15 us
  transfers between devices with their start and end apart: 4, of which 2 were waited for; matrix products, arithmetic and copies ran while one was open for 41% of the time, Pallas kernels for 0%

commit v1 on v0

v1 whole, which is shorter than its diff:
```python
import functools

import jax
import jax.numpy as jnp
from jax import lax
from jax.experimental import pallas as pl
from jax.experimental.pallas import tpu as pltpu
from jax.sharding import PartitionSpec as P


HD = 128
TB = 256
bf16 = jnp.bfloat16
f32 = jnp.float32


def nn(a, b):
    return lax.dot_general(a, b, (((1,), (0,)), ((), ())), preferred_element_type=f32)


def nt(a, b):
    return lax.dot_general(a, b, (((1,), (1,)), ((), ())), preferred_element_type=f32)


def tn(a, b):
    return lax.dot_general(a, b, (((0,), (0,)), ((), ())), preferred_element_type=f32)


def doc_start(info, docs, at):
    start = jnp.zeros_like(at)
    for i in range(docs):
        end = info[i]
        start = jnp.where(end <= at, end, start)
    return start


def col_iota(first):
    return first + lax.broadcasted_iota(jnp.int32, (TB, HD), 0)


def tail_kernel(info, a_ref, b_ref, out_ref, *, docs, heads, of_last):
    step = pl.program_id(0)

    @pl.when(step == 0)
    def _():
        out_ref[...] = jnp.zeros_like(out_ref)

    base = info[docs]
    first = base + step * TB
    at = col_iota(first)
    if of_last:
        match = at >= doc_start(info, docs, base + info[docs + 1] - 1)
    else:
        match = doc_start(info, docs, at) < base
    weight = match.astype(bf16)
    for h in range(heads):
        cols = slice(h * HD, (h + 1) * HD)
        out_ref[h] += tn(a_ref[:, cols] * weight, b_ref[:, cols])


def block_terms(info, docs, first):
    at = col_iota(first)
    start = doc_start(info, docs, at)
    last_start = doc_start(info, docs, first + TB - 1)
    first_match = start < first
    last_match = at >= last_start
    keep = jnp.where(last_start < first, 1.0, 0.0).astype(f32)
    return start, first_match, last_match, keep


def lower_mask(start, first):
    rows = lax.broadcasted_iota(jnp.int32, (TB, TB), 0)
    cols = lax.broadcasted_iota(jnp.int32, (TB, TB), 1)
    from_ = jnp.concatenate([start - first] * (TB // HD), axis=1)
    return (cols <= rows) & (cols >= from_)


def upper_mask(info, docs, first):
    rows = lax.broadcasted_iota(jnp.int32, (TB, TB), 0)
    cols = lax.broadcasted_iota(jnp.int32, (TB, TB), 1)
    start = doc_start(info, docs, first + lax.broadcasted_iota(jnp.int32, (1, TB), 1)) - first
    return (rows <= cols) & (rows >= start)


def forward_kernel(info, x_ref, k_ref, v_ref, carry_ref, *refs, docs, heads, flip, steps):
    outs, state = refs[:-1], refs[-1]
    step = pl.program_id(0)

    @pl.when(step == 0)
    def _():
        state[...] = carry_ref[...]

    first = info[docs] + step * TB
    start, first_match, last_match, keep = block_terms(info, docs, first)
    mask = lower_mask(start, first)
    first_weight = first_match.astype(bf16)
    last_weight = last_match.astype(bf16)
    for h in range(heads):
        cols = slice(h * HD, (h + 1) * HD)
        x, k, v = x_ref[:, cols], k_ref[:, cols], v_ref[:, cols]
        now = state[h]
        if flip:
            inner = jnp.where(mask, nt(x, v), 0.0).astype(bf16)
            out = nn(inner, k) + nt(x * first_weight, now.astype(bf16))
        else:
            inner = jnp.where(mask, nt(x, k), 0.0).astype(bf16)
            out = nn(inner, v) + nn(x * first_weight, now.astype(bf16))
        state[h] = keep * now + tn(k * last_weight, v)
        if flip:
            outs[0][:, cols] = out.astype(bf16)
            continue
        turned = out.T.astype(bf16)
        each = steps // len(outs)
        for i, out_ref in enumerate(outs):
            @pl.when(step // each == i)
            def _():
                out_ref[cols, :] = turned


def backward_kernel(info, q_ref, k_ref, v_ref, g_ref, carry_ref, dk_ref, dv_ref, state, *, docs, heads, steps):
    step = pl.program_id(0)

    @pl.when(step == 0)
    def _():
        state[...] = carry_ref[...]

    first = info[docs] + (steps - 1 - step) * TB
    _, first_match, last_match, keep = block_terms(info, docs, first)
    mask = upper_mask(info, docs, first)
    first_weight = first_match.astype(bf16)
    last_weight = last_match.astype(bf16)
    for h in range(heads):
        cols = slice(h * HD, (h + 1) * HD)
        q, k, v, g = q_ref[:, cols], k_ref[:, cols], v_ref[:, cols], g_ref[:, cols]
        now = state[h]
        low = now.astype(bf16)
        attn = jnp.where(mask, nt(k, q), 0.0).astype(bf16)
        pgrad = jnp.where(mask, nt(v, g), 0.0).astype(bf16)
        dk_ref[:, cols] = (nn(pgrad, q) + nt(v * last_weight, low)).astype(bf16)
        dv_ref[:, cols] = (nn(attn, g) + nn(k * last_weight, low)).astype(bf16)
        state[h] = keep * now + tn(q * first_weight, g)


def params():
    return pltpu.CompilerParams(dimension_semantics=("arbitrary",))


def cost(length, heads, matmuls, states, arrays):
    flops = length * heads * 2 * HD * (matmuls * TB + states * HD)
    return pl.CostEstimate(flops=flops, bytes_accessed=arrays * length * heads * HD * 2, transcendentals=0)


def device_state(info, a, b, docs, of_last):
    length, width = a.shape
    heads = width // HD
    spec = pl.BlockSpec((TB, width), lambda i, info: (i, 0))
    whole = pl.BlockSpec((heads, HD, HD), lambda i, info: (0, 0, 0))
    return pl.pallas_call(
        functools.partial(tail_kernel, docs=docs, heads=heads, of_last=of_last),
        out_shape=jax.ShapeDtypeStruct((heads, HD, HD), f32),
        grid_spec=pltpu.PrefetchScalarGridSpec(
            num_scalar_prefetch=1, grid=(length // TB,), in_specs=[spec, spec], out_specs=whole),
        compiler_params=params(), cost_estimate=cost(length, heads, 0, 1, 2),
    )(info, a, b)


def forward(info, x, k, v, carry, docs, flip, parts=1):
    length, width = x.shape
    heads = width // HD
    steps = length // TB
    each = steps // parts
    spec = pl.BlockSpec((TB, width), lambda i, info: (i, 0))
    whole = pl.BlockSpec((heads, HD, HD), lambda i, info: (0, 0, 0))
    if flip:
        out_shape, out_specs = (jax.ShapeDtypeStruct((length, width), bf16),), [spec]
    else:
        out_shape = (jax.ShapeDtypeStruct((width, length // parts), bf16),) * parts
        out_specs = [
            pl.BlockSpec((width, TB), lambda i, info, j=j: (0, jnp.clip(i - j * each, 0, each - 1)))
            for j in range(parts)]
    return pl.pallas_call(
        functools.partial(forward_kernel, docs=docs, heads=heads, flip=flip, steps=steps),
        out_shape=out_shape,
        grid_spec=pltpu.PrefetchScalarGridSpec(
            num_scalar_prefetch=1, grid=(steps,), in_specs=[spec, spec, spec, whole], out_specs=out_specs,
            scratch_shapes=[pltpu.VMEM((heads, HD, HD), f32)]),
        compiler_params=params(), cost_estimate=cost(length, heads, 2, 2, 4),
    )(info, x, k, v, carry)


def backward(info, q, k, v, g, carry, docs):
    length, width = q.shape
    heads = width // HD
    steps = length // TB
    spec = pl.BlockSpec((TB, width), lambda i, info: (steps - 1 - i, 0))
    whole = pl.BlockSpec((heads, HD, HD), lambda i, info: (0, 0, 0))
    return pl.pallas_call(
        functools.partial(backward_kernel, docs=docs, heads=heads, steps=steps),
        out_shape=(jax.ShapeDtypeStruct((length, width), bf16),) * 2,
        grid_spec=pltpu.PrefetchScalarGridSpec(
            num_scalar_prefetch=1, grid=(steps,), in_specs=[spec] * 4 + [whole], out_specs=[spec, spec],
            scratch_shapes=[pltpu.VMEM((heads, HD, HD), f32)]),
        compiler_params=params(), cost_estimate=cost(length, heads, 4, 3, 6), name="grad_kv",
    )(info, q, k, v, g, carry)


def carried(state, weights, before):
    count = lax.axis_size("seq")
    low = state.astype(bf16)
    total = jnp.zeros_like(state)
    for gap in range(1, count):
        if before:
            pairs = [(j, j + gap) for j in range(count - gap)]
        else:
            pairs = [(j + gap, j) for j in range(count - gap)]
        moved = lax.ppermute(low, "seq", pairs)
        total = total + weights[gap - 1] * moved.astype(f32)
    return total


def spread_kernel(at, *refs, terms, sums, outs):
    xs, ws = refs[:terms[0]], refs[terms[0]:terms[0] + terms[1]]
    bases = refs[terms[0] + terms[1]:-len(outs)]
    out_refs = refs[-len(outs):]
    for out_ref, products, base in zip(out_refs, outs, sums):
        total = None
        for i, j in products:
            term = nt(xs[i][...], ws[j][...])
            total = term if total is None else total + term
        for b in base:
            total = total + bases[b][...].astype(f32)
        out_ref[...] = total.astype(out_ref.dtype)


def spread(xs, ws, bases, outs, dtype, into=None, offset=0, size=None, block=512):
    depth = xs[0][0].shape[1]
    width = ws[0][0].shape[0]
    size = size or xs[0][0].shape[0]
    block = min(block, size)
    steps = size // block
    cols = jnp.stack([jnp.asarray(d, jnp.int32) for _, d in ws])
    x_specs = [pl.BlockSpec((block, depth), lambda i, at, f=f: (i + f, 0)) for _, f in xs]
    w_specs = [pl.BlockSpec((width, depth), lambda i, at, j=j: (0, at[j])) for j in range(len(ws))]
    b_specs = [pl.BlockSpec((block, width), lambda i, at, f=f: (i + f, 0)) for _, f in bases]
    length = size if into is None else into[0]
    out_spec = pl.BlockSpec((block, width), lambda i, at: (i + offset, 0))
    operands = [x for x, _ in xs] + [w for w, _ in ws] + [b for b, _ in bases]
    in_specs = x_specs + w_specs + b_specs
    alias = {}
    body = functools.partial(
        spread_kernel, terms=(len(xs), len(ws)), sums=[o[1] for o in outs], outs=[o[0] for o in outs])
    kernel = body
    if into is not None and into[1] is not None:
        alias = {1 + len(operands): 0}
        operands.append(into[1])
        in_specs = in_specs + [pl.BlockSpec(memory_space=pl.ANY)]
        extra = len(operands)

        def kernel(at, *refs):
            return body(at, *(refs[:extra - 1] + refs[extra:]))

    flops = sum(len(o[0]) for o in outs) * 2 * size * depth * width
    moved = 2 * (len(xs) * size * depth + len(ws) * width * depth) + 4 * (len(outs) + len(bases)) * size * width
    return pl.pallas_call(
        kernel,
        out_shape=tuple(jax.ShapeDtypeStruct((length, width), dtype) for _ in outs),
        grid_spec=pltpu.PrefetchScalarGridSpec(
            num_scalar_prefetch=1, grid=(steps,), in_specs=in_specs, out_specs=[out_spec] * len(outs)),
        compiler_params=params(), input_output_aliases=alias,
        cost_estimate=pl.CostEstimate(flops=flops, bytes_accessed=moved, transcendentals=0),
    )(cols, *operands)


def gather_kernel(*refs, lefts, parts):
    left, right, out_ref = refs[:lefts], refs[lefts:-1], refs[-1]
    total = None
    for i in range(parts):
        a, b = left[i * lefts // parts], right[i * len(right) // parts]
        ka, kb = a.shape[1] * lefts // parts, b.shape[0] * len(right) // parts
        ia, ib = i % (parts // lefts), i % (parts // len(right))
        term = nn(a[:, ia * ka:(ia + 1) * ka], b[ib * kb:(ib + 1) * kb, :])
        total = term if total is None else total + term
    out_ref[...] = total.astype(out_ref.dtype)


def weight_term(lefts, rights, block=256):
    width = lefts[0].shape[0]
    depth = rights[0].shape[1]
    block = min(block, depth)
    length = sum(x.shape[1] for x in lefts)
    return pl.pallas_call(
        functools.partial(gather_kernel, lefts=len(lefts), parts=max(len(lefts), len(rights))),
        out_shape=jax.ShapeDtypeStruct((width, depth), bf16),
        grid=(depth // block,),
        in_specs=[pl.BlockSpec(x.shape, lambda i: (0, 0)) for x in lefts]
        + [pl.BlockSpec((x.shape[0], block), lambda i: (0, i)) for x in rights],
        out_specs=pl.BlockSpec((width, block), lambda i: (0, i)),
        compiler_params=params(),
        cost_estimate=pl.CostEstimate(
            flops=2 * length * width * depth, bytes_accessed=2 * length * (width + depth), transcendentals=0),
    )(*lefts, *rights)


def row_start(ends, at):
    return jnp.max(jnp.where(ends <= at, ends, 0))


def gather_plan(c, w, values_of, rest_of):
    full = lax.all_gather(c, "head", axis=1, tiled=True)
    (attn_out,) = values_of(1)
    grads = nt(full, w).astype(bf16)
    outs = rest_of(grads)
    partial = nn(attn_out, full).astype(bf16)
    grad_w = lax.psum_scatter(partial, ("seq", "rep"), scatter_dimension=1, tiled=True)
    return outs, grad_w.astype(f32)


SWAP = [(0, 1), (1, 0), (2, 3), (3, 2)]
MIDDLE = [(1, 2), (2, 1)]
OUTWARD = [(1, 0), (2, 3)]
INWARD = [(0, 1), (3, 2)]


def line_plan(c, w, values_of, rest_of, pieces=4):
    me = lax.axis_index("head")
    length, depth = c.shape
    rows = w.shape[0]
    group = ("seq", "rep")
    count = lax.axis_size(group)
    part = rows // count

    def send(x, pairs):
        return lax.ppermute(x, "head", pairs)

    def scatter(x):
        return lax.psum_scatter(x, group, scatter_dimension=0, tiled=True)

    def columns(x, d):
        return lax.dynamic_slice_in_dim(x, d * depth, depth, 1)

    d_own, d_one, d_two, d_three = me, me ^ 1, 3 - me, (3 - me) ^ 1
    mine = lax.dynamic_slice_in_dim(w, lax.axis_index(group) * part, part, 0)
    far_w = jnp.concatenate([columns(mine, d_three), columns(mine, d_two)], axis=1)
    far_w = send(far_w, INWARD)
    far_w = lax.all_gather(far_w, group, axis=0, tiled=True)

    one = send(c, SWAP)
    two = send(c, MIDDLE)
    step = length // pieces
    three = [send(one[i * step:(i + 1) * step], MIDDLE) for i in range(pieces)]

    (own_sum,) = spread([(c, 0)], [(w, d_own)], [], [([(0, 0)], [])], f32)
    attn_out = values_of(2)
    far_out = [send(x, INWARD) for x in attn_out]
    terms = [weight_term(attn_out, [c])]
    near_sum, far_sum = spread(
        [(one, 0), (two, 0)], [(w, d_one), (w, d_two), (far_w, 0)], [(own_sum, 0)],
        [([(0, 0), (1, 1)], [0]), ([(1, 2)], [])], f32)
    terms += [weight_term(attn_out, [one]), weight_term(attn_out, [two])]
    far_grads = []
    for i in range(pieces):
        (x,) = spread([(three[i], 0)], [(far_w, 1)], [(far_sum, i)], [([(0, 0)], [0])], bf16)
        far_grads.append(send(x, OUTWARD))
    terms += [
        weight_term(attn_out, three),
        weight_term(far_out, [two]), weight_term(far_out, three)]
    grads = None
    for i in range(pieces):
        (grads,) = spread(
            [(three[i], 0)], [(w, d_three)], [(near_sum, i), (far_grads[i], 0)],
            [([(0, 0)], [0, 1])], bf16, into=(length, grads), offset=i)
    outs = rest_of(grads)

    terms = [scatter(x) for x in terms]
    sent = [send(x, OUTWARD) for x in terms[4:]]
    total = jnp.zeros((part, 4 * depth), bf16)
    for d, term in ((d_own, terms[0]), (d_one, terms[1]), (d_two, terms[2] + sent[1]), (d_three, terms[3] + sent[0])):
        total = lax.dynamic_update_slice_in_dim(total, term, d * depth, 1)
    grad_w = lax.all_to_all(total, group, split_axis=1, concat_axis=0, tiled=True)
    return outs, grad_w.astype(f32)


def on_device(query_heads, key_heads, value_heads, out_cotangent, out_weight, doc_ends):
    q, k, v, c = query_heads[0], key_heads[0], value_heads[0], out_cotangent[0]
    length = q.shape[0]
    ends = doc_ends[0].astype(jnp.int32)
    docs = ends.shape[0]
    here, count = lax.axis_index("seq"), lax.axis_size("seq")
    first = here * length
    last = first + length - 1
    info = jnp.concatenate([ends, jnp.stack([first, jnp.full_like(first, length)])]).astype(jnp.int32)

    before_start = row_start(ends, first - 1)
    before = [(before_start <= last - gap * length).astype(f32) for gap in range(1, count)]
    after = [(row_start(ends, first + gap * length - 1) <= last).astype(f32) for gap in range(1, count)]

    held = []

    def values_of(parts):
        tail = device_state(info, k, v, docs, True)
        held.append(carried(tail, before, True))
        return forward(info, q, k, v, held[0], docs, False, parts)

    def rest_of(grads):
        head = device_state(info, q, grads, docs, False)
        carry = carried(head, after, False)
        (dq,) = forward(info, grads, k, v, held[0], docs, True)
        dk, dv = backward(info, q, k, v, grads, carry, docs)
        return dq[None], dk[None], dv[None]

    plan = line_plan if lax.axis_size("head") == 4 else gather_plan
    outs, grad_w = plan(c, out_weight, values_of, rest_of)
    return outs + (grad_w,)


def solution(mesh):
    in_specs = (
        P("rep", "seq", "head"),
        P("rep", "seq", "head"),
        P("rep", "seq", "head"),
        P("rep", "seq", "head"),
        P("head", None),
        P("rep", None),
    )
    out_specs = (
        P("rep", "seq", "head"),
        P("rep", "seq", "head"),
        P("rep", "seq", "head"),
        P("head", ("seq", "rep")),
    )

    return jax.shard_map(on_device, mesh=mesh, in_specs=in_specs, out_specs=out_specs, check_vma=False)
```

time: 718 us -> 647 us (0.901)
  matrix products: 222 us -> 0 us
  Pallas kernels: 0 us -> 203 us
  local copies, waits for them, and re-layouts: 148 us -> 16.8 us
  waiting for transfers between devices: 273 us -> 349 us
  starting transfers between devices: 0.16 us -> 48 us
  other arithmetic: 34.7 us -> 8.84 us
  blocking collectives: 12.1 us -> 0 us
    ppermute x0 -> x21, waiting for transfers between devices: none -> 245 us  [the longest x15 237 us: send(): return lax.ppermute(x, 'head', pairs)]
    dot_general x18 -> x0, matrix products: 222 us -> none  [the longest x1 23.9 us: on_device(): lax.dot_general(full_cotangent, out_weight, (((1,), (1,)), ((), ())), pre...]
    all_gather x3 -> x1, waiting for transfers between devices: 216 us -> 0.01 us  [line_plan(): far_w = lax.all_gather(far_w, group, axis=0, tiled=True)]
    pallas_call x0 -> x21, Pallas kernels: none -> 203 us  [the longest x10 69.2 us: spread(): pl.pallas_call(kernel, out_shape=tuple((jax.ShapeDtypeStruct((length, wid...]
    reduce_scatter x0 -> x6, waiting for transfers between devices: none -> 104 us  [scatter(): return lax.psum_scatter(x, group, scatter_dimension=0, tiled=True)]
    psum x1 -> x0, waiting for transfers between devices: 55.8 us -> none  [on_device(): summed = lax.psum(partial_grad, ('seq', 'rep'))]
    ppermute x0 -> x21, starting transfers between devices: none -> 43.7 us  [the longest x15 31.7 us: send(): return lax.ppermute(x, 'head', pairs)]
    reshape x4 -> x0, local copies, waits for them, and re-layouts: 38.3 us -> none  [the longest x1 10.1 us: local_pass(): dq.reshape(shape)]
  transfers between devices with their start and end apart: 4 -> 29, of which waited for: 2 -> 9; matrix products, arithmetic and copies ran while one was open for 41% -> 3% of each run, Pallas kernels for 0% -> 32%
where the time goes in v1:
time: 647 us; the launch traced here: 644 us
  waiting for transfers between devices  349 us (54%)
  Pallas kernels  203 us (31%)
  starting transfers between devices  48 us (7%)
  between operations  18.4 us (3%)
  local copies, waits for them, and re-layouts  16.8 us (3%)
  other arithmetic  8.84 us (1%)
    ppermute x15, waiting for transfers between devices, send(): return lax.ppermute(x, 'head', pairs)  237 us
    reduce_scatter x6, waiting for transfers between devices, scatter(): return lax.psum_scatter(x, group, scatter_dimension=0, tiled=True)  104 us
    pallas_call x10, Pallas kernels, spread(): pl.pallas_call(kernel, out_shape=tuple((jax.ShapeDtypeStruct((length, wid...  69.2 us
    pallas_call x6, Pallas kernels, weight_term(): pl.pallas_call(functools.partial(gather_kernel, lefts=len(lefts), parts=m...  52.7 us
    pallas_call x2, Pallas kernels, forward(): pl.pallas_call(functools.partial(forward_kernel, docs=docs, heads=heads,...  44.9 us
    ppermute x15, starting transfers between devices, send(): return lax.ppermute(x, 'head', pairs)  31.7 us
    pallas_call x1, Pallas kernels, backward(): pl.pallas_call(functools.partial(backward_kernel, docs=docs, heads=heads,...  19.2 us
    pallas_call x2, Pallas kernels, device_state(): pl.pallas_call(functools.partial(tail_kernel, docs=docs, heads=heads, of_...  17.3 us
  transfers between devices with their start and end apart: 29, of which 9 were waited for; matrix products, arithmetic and copies ran while one was open for 3% of the time, Pallas kernels for 32%

profile of v1, /device:TPU:0, one launch (start us, length us, event | category | flops | bytes accessed | tf_op | source)
XLA Modules:
  0.0 644.0 jit_solution(6878477385082579514)
XLA Ops:
  13.6 11.1 %collective-permute-done.3 = bf16[128,2048]{1,0:T(8,128)(2,1)S(1)} collective-permute-done((bf16[128,2048]{1,0:T(8,128)(2,1)S(1)}, bf16[128,2048]{1,0:T(8,128)(2,1)S(1)}, u32[]{:S(2)}, u32[]{:S(2)}) %collective-permute-start.3) | collective-permute-done | bytes 524320 | tf_op jit(solution)/shard_map/ppermute | solution.py:333
  29.6 8.6 %shard_map.103 = f32[8,128,128]{2,1,0:T(8,128)} custom-call(s32[9]{0:T(128)} %pad_add_fusion.info, bf16[2048,1024]{1,0:T(8,128)(2,1)} %bitcast.21, bf16[2048,1024]{1,0:T(8,128)(2,1)} %bitcast.25), custom_call_target="tpu_custom_call" | custom-call | flops 536870912 | bytes 8388608 | tf_op jit(solution)/shard_map/pallas_call | solution.py:158
  53.5 7.3 %collective-permute-done.12 = bf16[8,128,128]{2,1,0:T(8,128)(2,1)S(1)} collective-permute-done((bf16[8,128,128]{2,1,0:T(8,128)(2,1)S(1)}, bf16[8,128,128]{2,1,0:T(8,128)(2,1)S(1)}, u32[]{:S(2)}, u32[]{:S(2)}) %collective-permute-start.12) | collective-permute-done | bytes 262176 | tf_op jit(solution)/shard_map/ppermute | solution.py:216
  62.5 31.4 %shard_map.106 = (bf16[1024,1024]{1,0:T(8,128)(2,1)}, bf16[1024,1024]{1,0:T(8,128)(2,1)}) custom-call(s32[9]{0:T(128)} %pad_add_fusion.info, bf16[2048,1024]{1,0:T(8,128)(2,1)} %bitcast.29, bf16[2048,1024]{1,0:T(8,128)(2,1)} %bitcast.22, bf16[2048,1024]{1,0:T(8,128)(2,1)} %bitcast.26, f32[8,128,128]{2,1,0:T(8,128)} %multiply_add_fusion.1.carry_ref), custom_call_target="tpu_custom_call" | custom-call | flops 3221225472 | bytes 16777216 | tf_op jit(solution)/shard_map/pallas_call | solution.py:181
  93.9 6.6 %collective-permute-start.17 = (bf16[1024,1024]{1,0:T(8,128)(2,1)}, bf16[1024,1024]{1,0:T(8,128)(2,1)S(1)}, u32[]{:S(2)}, u32[]{:S(2)}) collective-permute-start(bf16[1024,1024]{1,0:T(8,128)(2,1)} %get-tuple-element.14.refs_0_), channel_id=1, source_target_pairs={{0,2},{6,4},{1,3},{7,5},{8,10},{14,12},{9,11},{15,13},{16,18},{22,... | collective-permute-start | bytes 6291464 | tf_op jit(solution)/shard_map/ppermute | solution.py:333
  103.1 84.0 %collective-permute-done.17.refs_0_ = bf16[1024,1024]{1,0:T(8,128)(2,1)S(1)} collective-permute-done((bf16[1024,1024]{1,0:T(8,128)(2,1)}, bf16[1024,1024]{1,0:T(8,128)(2,1)S(1)}, u32[]{:S(2)}, u32[]{:S(2)}) %collective-permute-start.17) | collective-permute-done | bytes 2097184 | tf_op jit(solution)/shard_map/ppermute | solution.py:333
  187.1 42.1 %collective-permute-done.18.refs_1_ = bf16[1024,1024]{1,0:T(8,128)(2,1)} collective-permute-done((bf16[1024,1024]{1,0:T(8,128)(2,1)}, bf16[1024,1024]{1,0:T(8,128)(2,1)}, u32[]{:S(2)}, u32[]{:S(2)}) %collective-permute-start.18) | collective-permute-done | bytes 2097184 | tf_op jit(solution)/shard_map/ppermute | solution.py:333
  229.2 8.7 %shard_map.112 = bf16[1024,1024]{1,0:T(8,128)(2,1)} custom-call(bf16[1024,1024]{1,0:T(8,128)(2,1)} %copy-done.7, bf16[1024,1024]{1,0:T(8,128)(2,1)} %collective-permute-done.18.refs_1_, bf16[2048,1024]{1,0:T(8,128)(2,1)} %collective-permute-done.2.refs_1_.refs_2_), custom_call_target="tpu_custom_call" | custom-call | flops 4294967296 | bytes 8388608 | tf_op jit(solution)/shard_map/pallas_call | solution.py:291
  246.1 9.0 %shard_map.110 = bf16[1024,1024]{1,0:T(8,128)(2,1)} custom-call(bf16[1024,1024]{1,0:T(8,128)(2,1)} %copy-done.7, bf16[1024,1024]{1,0:T(8,128)(2,1)} %collective-permute-done.18.refs_1_, bf16[512,1024]{1,0:T(8,128)(2,1)} %collective-permute-done.9.refs_0_.refs_2_, bf16[512,1024]{1,0:T(8,128)(2,1)} %copy-done.2, bf16[512,1024]{1,0:T(8,128)(2,1)} %copy-done.1, ...), custom_call_target="tpu_custom_call" | custom-call | flops 4294967296 | bytes 8388608 | tf_op jit(solution)/shard_map/pallas_call | solution.py:291
  255.2 9.0 %shard_map.107 = bf16[1024,1024]{1,0:T(8,128)(2,1)} custom-call(bf16[1024,1024]{1,0:T(8,128)(2,1)} %get-tuple-element.14.refs_0_, bf16[1024,1024]{1,0:T(8,128)(2,1)} %get-tuple-element.15.refs_1_, bf16[2048,1024]{1,0:T(8,128)(2,1)} %bitcast.35), custom_call_target="tpu_custom_call" | custom-call | flops 4294967296 | bytes 8388608 | tf_op jit(solution)/shard_map/pallas_call | solution.py:291
  264.2 8.7 %shard_map.108 = bf16[1024,1024]{1,0:T(8,128)(2,1)} custom-call(bf16[1024,1024]{1,0:T(8,128)(2,1)} %get-tuple-element.14.refs_0_, bf16[1024,1024]{1,0:T(8,128)(2,1)} %get-tuple-element.15.refs_1_, bf16[2048,1024]{1,0:T(8,128)(2,1)} %collective-permute-done.refs_0_.refs_2_), custom_call_target="tpu_custom_call" | custom-call | flops 4294967296 | bytes 8388608 | tf_op jit(solution)/shard_map/pallas_call | solution.py:291
  273.0 8.7 %shard_map.111 = bf16[1024,1024]{1,0:T(8,128)(2,1)} custom-call(bf16[1024,1024]{1,0:T(8,128)(2,1)} %get-tuple-element.14.refs_0_, bf16[1024,1024]{1,0:T(8,128)(2,1)} %get-tuple-element.15.refs_1_, bf16[512,1024]{1,0:T(8,128)(2,1)} %collective-permute-done.9.refs_0_.refs_2_, bf16[512,1024]{1,0:T(8,128)(2,1)} %copy-done.2, bf16[512,1024]{1,0:T(8,128)(2,1)} %copy-done.1, ...), custom_call_target="tpu_custom_call" | custom-call | flops 4294967296 | bytes 8388608 | tf_op jit(solution)/shard_map/pallas_call | solution.py:291
  282.0 8.6 %shard_map.109 = bf16[1024,1024]{1,0:T(8,128)(2,1)} custom-call(bf16[1024,1024]{1,0:T(8,128)(2,1)} %get-tuple-element.14.refs_0_, bf16[1024,1024]{1,0:T(8,128)(2,1)} %get-tuple-element.15.refs_1_, bf16[2048,1024]{1,0:T(8,128)(2,1)} %collective-permute-done.2.refs_1_.refs_2_), custom_call_target="tpu_custom_call" | custom-call | flops 4294967296 | bytes 8388608 | tf_op jit(solution)/shard_map/pallas_call | solution.py:291
  291.3 9.3 %shard_map.93.refs_5_ = f32[2048,1024]{1,0:T(8,128)} custom-call(s32[1]{0:T(128)} %bitcast.6.at, bf16[2048,1024]{1,0:T(8,128)(2,1)} %bitcast.36, bf16[1024,4096]{1,0:T(8,128)(2,1)} %refs_1_.9), custom_call_target="tpu_custom_call" | custom-call | flops 4294967296 | bytes 14680064 | tf_op jit(solution)/shard_map/pallas_call | solution.py:264
  300.5 20.3 %shard_map.94 = (f32[2048,1024]{1,0:T(8,128)}, f32[2048,1024]{1,0:T(8,128)}) custom-call(s32[3]{0:T(128)} %pad_add_fusion.1.at, bf16[2048,1024]{1,0:T(8,128)(2,1)} %collective-permute-done.refs_0_.refs_2_, bf16[2048,1024]{1,0:T(8,128)(2,1)} %collective-permute-done.2.refs_1_.refs_2_, bf16[1024,4096]{1,0:T(8,128)(2,1)} %refs_1_.9, ...), custom_call_target="tpu_custom_call" | custom-call | flops 12884901888 | bytes 39845888 | tf_op jit(solution)/shard_map/pallas_call | solution.py:264
  346.6 99.4 %collective-permute-done.20 = bf16[128,1024]{1,0:T(8,128)(2,1)S(1)} collective-permute-done((bf16[128,1024]{1,0:T(8,128)(2,1)}, bf16[128,1024]{1,0:T(8,128)(2,1)S(1)}, u32[]{:S(2)}, u32[]{:S(2)}) %collective-permute-start.20) | collective-permute-done | bytes 262176 | tf_op jit(solution)/shard_map/ppermute | solution.py:333
  452.2 18.1 %reduce-scatter.9.cloned.1.call-done = bf16[128,1024]{1,0:T(8,128)(2,1)} async-done(((bf16[1024,1024]{1,0:T(8,128)(2,1)}), bf16[128,1024]{1,0:T(8,128)(2,1)}) %reduce-scatter.9.cloned.1.call-update) | async-done | bytes 262160 | tf_op jit(solution)/shard_map/reduce_scatter | solution.py:336
  472.2 42.4 %reduce-scatter.15.cloned.1.call-done = bf16[128,1024]{1,0:T(8,128)(2,1)} async-done(((bf16[1024,1024]{1,0:T(8,128)(2,1)}), bf16[128,1024]{1,0:T(8,128)(2,1)}) %reduce-scatter.15.cloned.1.call-update) | async-done | bytes 262160 | tf_op jit(solution)/shard_map/reduce_scatter | solution.py:336
  515.8 43.2 %reduce-scatter.11.cloned.1.call-done = bf16[128,1024]{1,0:T(8,128)(2,1)} async-done(((bf16[1024,1024]{1,0:T(8,128)(2,1)}), bf16[128,1024]{1,0:T(8,128)(2,1)}) %reduce-scatter.11.cloned.1.call-update) | async-done | bytes 262160 | tf_op jit(solution)/shard_map/reduce_scatter | solution.py:336
  566.4 5.2 shard_map.99.refs_4_
  571.6 5.1 shard_map.100.refs_4_
  587.8 8.7 %shard_map.105 = f32[8,128,128]{2,1,0:T(8,128)} custom-call(s32[9]{0:T(128)} %pad_add_fusion.info, bf16[2048,1024]{1,0:T(8,128)(2,1)} %bitcast.30, bf16[2048,1024]{1,0:T(8,128)(2,1)} %shard_map.102.x_ref.b_ref.g_ref), custom_call_target="tpu_custom_call" | custom-call | flops 536870912 | bytes 8388608 | tf_op jit(solution)/shard_map/pallas_call | solution.py:158
  601.5 13.6 %shard_map.104 = bf16[2048,1024]{1,0:T(8,128)(2,1)} custom-call(s32[9]{0:T(128)} %pad_add_fusion.info, bf16[2048,1024]{1,0:T(8,128)(2,1)} %shard_map.102.x_ref.b_ref.g_ref, bf16[2048,1024]{1,0:T(8,128)(2,1)} %bitcast.23, bf16[2048,1024]{1,0:T(8,128)(2,1)} %bitcast.27, f32[8,128,128]{2,1,0:T(8,128)} %multiply_add_fusion.1.carry_ref), custom_call_target="tpu_custom_call" | custom-call | flops 3221225472 | bytes 16777216 | tf_op jit(solution)/shard_map/pallas_call | solution.py:181
  616.0 19.2 %grad_kv.1 = (bf16[2048,1024]{1,0:T(8,128)(2,1)}, bf16[2048,1024]{1,0:T(8,128)(2,1)}) custom-call(s32[9]{0:T(128)} %pad_add_fusion.info, bf16[2048,1024]{1,0:T(8,128)(2,1)} %bitcast.31, bf16[2048,1024]{1,0:T(8,128)(2,1)} %bitcast.24, bf16[2048,1024]{1,0:T(8,128)(2,1)} %bitcast.28, bf16[2048,1024]{1,0:T(8,128)(2,1)} %shard_map.102.x_ref.b_ref.g_ref, ...), custom_call_target="tpu_custom_call" | custom-call | flops 5905580032 | bytes 25165824 | tf_op jit(solution)/shard_map/grad_kv/pallas_call | solution.py:197
  (101 shorter events, 97.3 us)
Async XLA Ops:
  7.2 293.4 %all-gather.2.cloned.1.call-start = ((), (), s32[]{:S(2)}) async-start(), calls=%async_computation.7 | async-start | bytes 4718592 | tf_op jit(solution)/shard_map/all_gather | solution.py:345
  8.6 16.1 %collective-permute-start.3 = (bf16[128,2048]{1,0:T(8,128)(2,1)S(1)}, bf16[128,2048]{1,0:T(8,128)(2,1)S(1)}, u32[]{:S(2)}, u32[]{:S(2)}) collective-permute-start(bf16[128,2048]{1,0:T(8,128)(2,1)S(1)} %pad_maximum_fusion), channel_id=1, source_target_pairs={{0,2},{6,4},{1,3},{7,5},{8,10},{14,12},{9,11},{15,13},{16,18},{22,... | collective-permute-start | bytes 1572872 | tf_op jit(solution)/shard_map/ppermute | solution.py:333
  25.6 301.4 %reduce-scatter.17.cloned.1.call-start = ((), (), s32[]{:S(2)}) async-start(), calls=%async_computation.13 | async-start | bytes 2359296 | tf_op jit(solution)/shard_map/reduce_scatter | solution.py:336
  25.6 203.6 %collective-permute-start.2 = (bf16[2048,1024]{1,0:T(8,128)(2,1)}, bf16[2048,1024]{1,0:T(8,128)(2,1)}, u32[]{:S(2)}, u32[]{:S(2)}) collective-permute-start(bf16[2048,1024]{1,0:T(8,128)(2,1)} %bitcast.33), channel_id=1, source_target_pairs={{2,4},{4,2},{3,5},{5,3},{10,12},{12,10},{11,13},{13,11},{18,20},{2... | collective-permute-start | bytes 12582920 | tf_op jit(solution)/shard_map/ppermute | solution.py:333
  43.7 17.2 %collective-permute-start.12 = (bf16[8,128,128]{2,1,0:T(8,128)(2,1)S(1)}, bf16[8,128,128]{2,1,0:T(8,128)(2,1)S(1)}, u32[]{:S(2)}, u32[]{:S(2)}) collective-permute-start(bf16[8,128,128]{2,1,0:T(8,128)(2,1)S(1)} %convert_element_type.52), channel_id=1, source_target_pairs={{0,16},{8,24},{1,17},{9,25},{2,18},{10,26},{3,19},{11,27},{4,20},{... | collective-permute-start | bytes 786440 | tf_op jit(solution)/shard_map/ppermute | solution.py:216
  45.0 16.6 %collective-permute-start.11 = (bf16[8,128,128]{2,1,0:T(8,128)(2,1)S(1)}, bf16[8,128,128]{2,1,0:T(8,128)(2,1)S(1)}, u32[]{:S(2)}, u32[]{:S(2)}) collective-permute-start(bf16[8,128,128]{2,1,0:T(8,128)(2,1)S(1)} %convert_element_type.52), channel_id=1, source_target_pairs={{0,8},{8,16},{16,24},{1,9},{9,17},{17,25},{2,10},{10,18},{18,26},{... | collective-permute-start | bytes 786440 | tf_op jit(solution)/shard_map/ppermute | solution.py:216
  47.5 190.5 %collective-permute-start = (bf16[2048,1024]{1,0:T(8,128)(2,1)}, bf16[2048,1024]{1,0:T(8,128)(2,1)}, u32[]{:S(2)}, u32[]{:S(2)}) collective-permute-start(bf16[2048,1024]{1,0:T(8,128)(2,1)} %bitcast.34), channel_id=1, source_target_pairs={{0,2},{2,0},{4,6},{6,4},{1,3},{3,1},{5,7},{7,5},{8,10},{10,8},{12,... | collective-permute-start | bytes 12582920 | tf_op jit(solution)/shard_map/ppermute | solution.py:333
  93.9 93.2 %collective-permute-start.17 = (bf16[1024,1024]{1,0:T(8,128)(2,1)}, bf16[1024,1024]{1,0:T(8,128)(2,1)S(1)}, u32[]{:S(2)}, u32[]{:S(2)}) collective-permute-start(bf16[1024,1024]{1,0:T(8,128)(2,1)} %get-tuple-element.14.refs_0_), channel_id=1, source_target_pairs={{0,2},{6,4},{1,3},{7,5},{8,10},{14,12},{9,11},{15,13},{16,18},{22,... | collective-permute-start | bytes 6291464 | tf_op jit(solution)/shard_map/ppermute | solution.py:333
  100.5 128.8 %collective-permute-start.18 = (bf16[1024,1024]{1,0:T(8,128)(2,1)}, bf16[1024,1024]{1,0:T(8,128)(2,1)}, u32[]{:S(2)}, u32[]{:S(2)}) collective-permute-start(bf16[1024,1024]{1,0:T(8,128)(2,1)} %get-tuple-element.15.refs_1_), channel_id=1, source_target_pairs={{0,2},{6,4},{1,3},{7,5},{8,10},{14,12},{9,11},{15,13},{16,18},{22,... | collective-permute-start | bytes 6291464 | tf_op jit(solution)/shard_map/ppermute | solution.py:333
  237.9 208.1 %reduce-scatter.13.cloned.1.call-start = ((), (), s32[]{:S(2)}) async-start(), calls=%async_computation.11 | async-start | bytes 2359296 | tf_op jit(solution)/shard_map/reduce_scatter | solution.py:336
  255.1 194.1 %reduce-scatter.7.cloned.1.call-start = ((), (), s32[]{:S(2)}) async-start(), calls=%async_computation.8 | async-start | bytes 2359296 | tf_op jit(solution)/shard_map/reduce_scatter | solution.py:336
  264.2 206.2 %reduce-scatter.9.cloned.1.call-start = ((), (), s32[]{:S(2)}) async-start(), calls=%async_computation.9 | async-start | bytes 2359296 | tf_op jit(solution)/shard_map/reduce_scatter | solution.py:336
  273.0 241.6 %reduce-scatter.15.cloned.1.call-start = ((), (), s32[]{:S(2)}) async-start(), calls=%async_computation.12 | async-start | bytes 2359296 | tf_op jit(solution)/shard_map/reduce_scatter | solution.py:336
  281.8 277.2 %reduce-scatter.11.cloned.1.call-start = ((), (), s32[]{:S(2)}) async-start(), calls=%async_computation.10 | async-start | bytes 2359296 | tf_op jit(solution)/shard_map/reduce_scatter | solution.py:336
  325.7 239.8 %collective-permute-start.10 = (bf16[512,1024]{1,0:T(8,128)(2,1)}, bf16[512,1024]{1,0:T(8,128)(2,1)S(1)}, u32[]{:S(2)}, u32[]{:S(2)}) collective-permute-start(bf16[512,1024]{1,0:T(8,128)(2,1)} %shard_map.98), channel_id=1, source_target_pairs={{2,0},{4,6},{3,1},{5,7},{10,8},{12,14},{11,9},{13,15},{18,16},{20,... | collective-permute-start | bytes 3145736 | tf_op jit(solution)/shard_map/ppermute | solution.py:333
  327.0 119.0 %collective-permute-start.20 = (bf16[128,1024]{1,0:T(8,128)(2,1)}, bf16[128,1024]{1,0:T(8,128)(2,1)S(1)}, u32[]{:S(2)}, u32[]{:S(2)}) collective-permute-start(bf16[128,1024]{1,0:T(8,128)(2,1)} %reduce-scatter.17.cloned.1.call-done), channel_id=1, source_target_pairs={{2,0},{4,6},{3,1},{5,7},{10,8},{12,14},{11,9},{13,15},{18,16},{20,... | collective-permute-start | bytes 786440 | tf_op jit(solution)/shard_map/ppermute | solution.py:333
  333.1 238.5 %collective-permute-start.8 = (bf16[512,1024]{1,0:T(8,128)(2,1)}, bf16[512,1024]{1,0:T(8,128)(2,1)}, u32[]{:S(2)}, u32[]{:S(2)}) collective-permute-start(bf16[512,1024]{1,0:T(8,128)(2,1)} %shard_map.97), channel_id=1, source_target_pairs={{2,0},{4,6},{3,1},{5,7},{10,8},{12,14},{11,9},{13,15},{18,16},{20,... | collective-permute-start | bytes 3145736 | tf_op jit(solution)/shard_map/ppermute | solution.py:333
  339.2 237.5 %collective-permute-start.6 = (bf16[512,1024]{1,0:T(8,128)(2,1)}, bf16[512,1024]{1,0:T(8,128)(2,1)}, u32[]{:S(2)}, u32[]{:S(2)}) collective-permute-start(bf16[512,1024]{1,0:T(8,128)(2,1)} %shard_map.96), channel_id=1, source_target_pairs={{2,0},{4,6},{3,1},{5,7},{10,8},{12,14},{11,9},{13,15},{18,16},{20,... | collective-permute-start | bytes 3145736 | tf_op jit(solution)/shard_map/ppermute | solution.py:333
  345.3 236.5 %collective-permute-start.4 = (bf16[512,1024]{1,0:T(8,128)(2,1)}, bf16[512,1024]{1,0:T(8,128)(2,1)S(1)}, u32[]{:S(2)}, u32[]{:S(2)}) collective-permute-start(bf16[512,1024]{1,0:T(8,128)(2,1)} %shard_map.95), channel_id=1, source_target_pairs={{2,0},{4,6},{3,1},{5,7},{10,8},{12,14},{11,9},{13,15},{18,16},{20,... | collective-permute-start | bytes 3145736 | tf_op jit(solution)/shard_map/ppermute | solution.py:333
  446.0 113.1 %collective-permute-start.19 = (bf16[128,1024]{1,0:T(8,128)(2,1)}, bf16[128,1024]{1,0:T(8,128)(2,1)S(1)}, u32[]{:S(2)}, u32[]{:S(2)}) collective-permute-start(bf16[128,1024]{1,0:T(8,128)(2,1)} %reduce-scatter.13.cloned.1.call-done), channel_id=1, source_target_pairs={{2,0},{4,6},{3,1},{5,7},{10,8},{12,14},{11,9},{13,15},{18,16},{20,... | collective-permute-start | bytes 786440 | tf_op jit(solution)/shard_map/ppermute | solution.py:333
  561.7 73.5 %all-to-all-start = ((bf16[128,8,512]{0,2,1:T(8,128)(2,1)}), bf16[128,8,512]{0,2,1:T(8,128)(2,1)S(1)}, u32[]{:S(2)}, u32[]{:S(2)}) async-start(bf16[128,8,512]{0,2,1:T(8,128)(2,1)} %bitcast.13), calls=%async_computation.6 | async-start | bytes 2097152 | tf_op jit(solution)/shard_map/all_to_all | solution.py:379
  597.6 17.5 %collective-permute-start.16 = (bf16[8,128,128]{2,1,0:T(8,128)(2,1)S(1)}, bf16[8,128,128]{2,1,0:T(8,128)(2,1)S(1)}, u32[]{:S(2)}, u32[]{:S(2)}) collective-permute-start(bf16[8,128,128]{2,1,0:T(8,128)(2,1)S(1)} %convert_element_type.59), channel_id=1, source_target_pairs={{24,0},{25,1},{26,2},{27,3},{28,4},{29,5},{30,6},{31,7}} | collective-permute-start | bytes 786440 | tf_op jit(solution)/shard_map/ppermute | solution.py:216
  598.9 16.2 %collective-permute-start.15 = (bf16[8,128,128]{2,1,0:T(8,128)(2,1)S(1)}, bf16[8,128,128]{2,1,0:T(8,128)(2,1)S(1)}, u32[]{:S(2)}, u32[]{:S(2)}) collective-permute-start(bf16[8,128,128]{2,1,0:T(8,128)(2,1)S(1)} %convert_element_type.59), channel_id=1, source_target_pairs={{16,0},{24,8},{17,1},{25,9},{18,2},{26,10},{19,3},{27,11},{20,4},{... | collective-permute-start | bytes 786440 | tf_op jit(solution)/shard_map/ppermute | solution.py:216
  600.2 14.9 %collective-permute-start.14 = (bf16[8,128,128]{2,1,0:T(8,128)(2,1)S(1)}, bf16[8,128,128]{2,1,0:T(8,128)(2,1)S(1)}, u32[]{:S(2)}, u32[]{:S(2)}) collective-permute-start(bf16[8,128,128]{2,1,0:T(8,128)(2,1)S(1)} %convert_element_type.59), channel_id=1, source_target_pairs={{8,0},{16,8},{24,16},{9,1},{17,9},{25,17},{10,2},{18,10},{26,18},{... | collective-permute-start | bytes 786440 | tf_op jit(solution)/shard_map/ppermute | solution.py:216
  (13 other events, 95.5 us)
Sparse Core Ops, SparseCore 0:
  25.7 40.8 all-gather.1
  238.0 39.3 reduce-scatter.16
  280.7 99.8 reduce-scatter.12
  384.3 41.0 reduce-scatter.6
  429.2 41.0 reduce-scatter.8
  473.5 41.0 reduce-scatter.14
  517.9 41.1 reduce-scatter.10
